TPU v7x, 32 devices: a whole 2x2x4 slice. The times are simulated.
32 devices in a mesh: groups: 2 (over y), dp: 4 (over x, core), mp: 4 (over z).
Axes of the slice: x: 2, y: 2, z: 4, core: 2. Of those that a mesh axis runs over, the one named last changes fastest.
Arguments:
- base_states: bfloat16 [1280, 4096], P(('groups', 'dp'), 'mp'), parts along dimension 0, may hold values from -6 to 6
- source_states: bfloat16 [1280, 4096], P(('groups', 'dp'), 'mp'), parts along dimension 0, may hold values from -6 to 6
- source_rank: int32 [1280, 1], P(('groups', 'dp')), parts along dimension 0, may hold values from 0 to 3; in each aligned block of 160 rows (0 to 159, 160 to 319, ...) at most 80 rows name the same one
- source_row: int32 [1280], P(('groups', 'dp')), parts along dimension 0, may hold values from 0 to 159
- rotation: bfloat16 [4096, 4096], P(None, 'mp'), may hold values from -0.125 to 0.125
- mask_logits: float32 [4096], P('mp'), may hold values from -8 to 8
- norm_gain: bfloat16 [4096], replicated, may hold values from 0.25 to 1.75
- gate_weight: bfloat16 [4096, 14336], P(None, 'mp'), may hold values from -0.09375 to 0.09375
- up_weight: bfloat16 [4096, 14336], P(None, 'mp'), may hold values from -0.09375 to 0.09375
- hidden_cot: bfloat16 [1280, 14336], P(('groups', 'dp'), 'mp'), parts along dimension 0, may hold values from -0.23632812 to 0.23632812
Outputs:
- rotation_grad: float32 [8192, 4096], P(('groups', 'dp'), 'mp'), parts along dimension 0
- interchanged: bfloat16 [1280, 4096], P(('groups', 'dp'), 'mp'), parts along dimension 0
There are 2 independent parts, one for each index of `groups`. A program takes and returns all parts, laid end to end along the dimension named above; an argument that names none is the same for every part. Nothing has to cross between parts.
Inputs may be any that keep to these rules, and one draw needn't show every extreme that they name: `source_rank`: within the 160 tokens of each dp index, no dp index is named more than 80 times, and some dp index is named exactly 80 times by the tokens of some dp index.
All inputs are finite; a program needn't handle non-finite values.
Results may differ from a plain program's by a relative error of at most 0.014.
Values may be sent and summed in bfloat16 or wider, within the bound.
A program may use at most 192 MiB of HBM per device.

v0:
```python
import jax
import jax.numpy as jnp
from jax import lax
from jax.sharding import PartitionSpec as P


def contract_first(left, right):
    return lax.dot_general(
        left, right, (((0,), (0,)), ((), ())), preferred_element_type=jnp.float32
    )


def contract_last(left, right):
    return lax.dot_general(
        left, right, (((1,), (1,)), ((), ())), preferred_element_type=jnp.float32
    )


def shards(
    base_states,
    source_states,
    source_rank,
    source_row,
    rotation,
    mask_logits,
    norm_gain,
    gate_weight,
    up_weight,
    hidden_cot,
):
    tokens = base_states.shape[0]
    width = rotation.shape[0]
    ranks_of = source_rank[:, 0]
    everyone = lax.all_gather(source_states, "dp", axis=0, tiled=True)
    paired = jnp.take(everyone, ranks_of * tokens + source_row, axis=0)
    diff_local = (paired.astype(jnp.float32) - base_states.astype(jnp.float32)).astype(jnp.bfloat16)
    diff_full = lax.all_gather(diff_local, "mp", axis=1, tiled=True)
    mask = jax.nn.sigmoid(mask_logits)[None, :]
    coords = jnp.dot(diff_full, rotation, preferred_element_type=jnp.float32)
    weighted = (mask * coords).astype(jnp.bfloat16)
    moved = lax.psum_scatter(
        contract_last(rotation, weighted), "mp", scatter_dimension=0, tiled=True
    ).T
    interchanged = (base_states.astype(jnp.float32) + moved).astype(jnp.bfloat16)
    full_rows = lax.all_gather(interchanged, "mp", axis=1, tiled=True)
    states = full_rows.astype(jnp.float32)
    gain_f = norm_gain.astype(jnp.float32)[None, :]
    recip = lax.rsqrt(jnp.mean(states * states, axis=1, keepdims=True) + 1e-05)
    normed = (states * recip * gain_f).astype(jnp.bfloat16)
    gate = jnp.dot(normed, gate_weight, preferred_element_type=jnp.float32)
    up_val = jnp.dot(normed, up_weight, preferred_element_type=jnp.float32)
    sigm = jax.nn.sigmoid(gate)
    cotan = hidden_cot.astype(jnp.float32)
    dgate = (cotan * up_val * sigm * (1.0 + gate * (1.0 - sigm))).astype(jnp.bfloat16)
    dup_val = (cotan * gate * sigm).astype(jnp.bfloat16)
    partial_grad = contract_last(dgate, gate_weight) + contract_last(dup_val, up_weight)
    dnormed = lax.psum(partial_grad, "mp")
    scaled = gain_f * dnormed
    stat = jnp.sum(scaled * states, axis=1, keepdims=True)
    dinter = (recip * scaled - states * recip * recip * recip * stat / width).astype(jnp.bfloat16)
    coupled = (mask * jnp.dot(dinter, rotation, preferred_element_type=jnp.float32)).astype(
        jnp.bfloat16
    )
    rotation_grad = lax.psum_scatter(
        (contract_first(dinter, weighted) + contract_first(diff_full, coupled)).astype(
            jnp.bfloat16
        ),
        "dp",
        scatter_dimension=0,
        tiled=True,
    ).astype(jnp.float32)
    return (rotation_grad, interchanged)


def solution(mesh):
    placed = (
        P(("groups", "dp"), "mp"),
        P(("groups", "dp"), "mp"),
        P(("groups", "dp"), None),
        P(("groups", "dp")),
        P(None, "mp"),
        P("mp"),
        P(),
        P(None, "mp"),
        P(None, "mp"),
        P(("groups", "dp"), "mp"),
    )
    return jax.shard_map(
        shards,
        mesh=mesh,
        in_specs=placed,
        out_specs=(P(("groups", "dp"), "mp"), P(("groups", "dp"), "mp")),
        check_vma=False,
    )
```

profile of v0, /device:TPU:0, one launch (start us, length us, event | category | flops | bytes accessed | tf_op | source)
XLA Modules:
  0.0 437.6 jit_solution(6503187175433024214)
XLA Ops:
  7.2 0.0 copy-start.3
  7.2 0.0 copy-start.5
  7.2 0.0 all-gather.4.cloned.1.call-start
  7.2 0.7 all-gather.4.cloned.1.call-update
  7.9 0.0 all-gather.6.cloned.1.call-start
  8.0 0.7 broadcast_multiply_fusion
  8.6 0.7 compare_and_fusion
  9.3 21.2 %all-gather.4.cloned.1.call-done = bf16[640,1024]{1,0:T(8,128)(2,1)} async-done(((bf16[160,1024]{1,0:T(8,128)(2,1)}), bf16[640,1024]{1,0:T(8,128)(2,1)}) %all-gather.4.cloned.1.call-update) | async-done | bytes 1310736 | tf_op jit(solution)/shard_map/all_gather | solution.py:34
  30.5 2.7 gather_fusion
  33.2 0.0 copy-done.3
  33.2 0.9 fusion.25
  34.1 0.0 all-gather.6.cloned.1.call-update
  34.1 0.0 reduce-scatter.3.cloned.1.call-start
  34.1 0.0 copy-done.5
  34.2 32.8 %all-gather.6.cloned.1.call-done = bf16[160,4096]{1,0:T(8,128)(2,1)} async-done(((bf16[160,1024]{1,0:T(8,128)(2,1)}), bf16[160,4096]{1,0:T(8,128)(2,1)}) %all-gather.6.cloned.1.call-update) | async-done | bytes 1310736 | tf_op jit(solution)/shard_map/all_gather | solution.py:37
  66.9 5.3 %fusion.20 = bf16[160,1024]{1,0:T(8,128)(2,1)S(1)} fusion(bf16[160,4096]{1,0:T(8,128)(2,1)} %all-gather.6.cloned.1.call-done, bf16[4096,1024]{1,0:T(8,128)(2,1)} %param.14, f32[1024]{0:T(1024)S(1)} %add_divide_fusion.2), kind=kOutput, calls=%fused_computation.32 | convolution fusion | flops 1342504960 | bytes 10031104 | tf_op jit(solution)/shard_map/dot_general | solution.py:39
  72.3 7.8 %convolution_bitcast_fusion = f32[4096,160]{0,1:T(8,128)} fusion(bf16[160,1024]{1,0:T(8,128)(2,1)S(1)} %fusion.20, bf16[4096,1024]{1,0:T(8,128)(2,1)} %param.14), kind=kOutput, calls=%fused_computation.5 | convolution fusion | flops 1342177280 | bytes 11337728 | tf_op jit(solution)/shard_map/dot_general | solution.py:14
  80.1 0.0 copy-start.4
  80.1 0.0 reduce-scatter.3.cloned.1.call-update
  80.1 0.0 all-gather.8.cloned.1.call-start
  80.1 51.2 %reduce-scatter.3.cloned.1.call-done = f32[1024,160]{0,1:T(8,128)} async-done(((f32[4096,160]{0,1:T(8,128)}), f32[1024,160]{0,1:T(8,128)}) %reduce-scatter.3.cloned.1.call-update) | async-done | bytes 655376 | tf_op jit(solution)/shard_map/reduce_scatter | solution.py:41
  131.3 1.9 fusion.26
  133.2 0.0 all-gather.8.cloned.1.call-update
  133.3 0.2 all-reduce.2.cloned.1.call-start
  133.5 0.0 copy-done.4
  133.5 32.3 %all-gather.8.cloned.1.call-done = bf16[160,4096]{1,0:T(8,128)(2,1)} async-done(((bf16[160,1024]{1,0:T(8,128)(2,1)}), bf16[160,4096]{1,0:T(8,128)(2,1)}) %all-gather.8.cloned.1.call-update) | async-done | bytes 1310736 | tf_op jit(solution)/shard_map/all_gather | solution.py:45
  165.8 1.7 fusion.13
  167.5 0.0 copy-start
  167.5 0.0 copy-start.6
  167.5 16.2 %fusion.27 = f32[160,3584]{1,0:T(8,128)} fusion(bf16[4096,3584]{1,0:T(8,128)(2,1)} %param.17, bf16[160,4096]{1,0:T(8,128)(2,1)} %all-gather.8.cloned.1.call-done, f32[4096]{0:T(1024)S(1)} %convert_element_type.52, f32[160]{0:T(256)S(1)} %add_rsqrt_fusion), kind=kOutput, calls=%fused_computation.40 | convolution fusion | flops 4700241920 | bytes 32981632 | tf_op jit(solution)/shard_map/dot_general | solution.py:50
  183.7 0.0 copy-done
  183.7 0.0 copy-done.6
  183.7 25.1 %fusion.3 = f32[160,4096]{1,0:T(8,128)} fusion(bf16[4096,3584]{1,0:T(8,128)(2,1)} %param.17, bf16[4096,3584]{1,0:T(8,128)(2,1)} %param.18, bf16[160,3584]{1,0:T(8,128)(2,1)S(1)} %copy-done.6, f32[160,3584]{1,0:T(8,128)} %fusion.27, bf16[160,4096]{1,0:T(8,128)(2,1)S(1)} %copy-done, f32[4096]{0:T(1024)S(1)} %convert_element_type.52, f32[160]{0:T(256)S(1)} %add_rsqrt_fusion), kind=kOutput, calls=%fused_computation.11 | convolution fusion | flops 9404170240 | bytes 66110080 | tf_op jit(solution)/shard_map/dot_general | solution.py:14
  208.8 16.1 %convolution_add_fusion = f32[160,4096]{1,0:T(8,128)} fusion(f32[160,4096]{1,0:T(8,128)} %fusion.3, bf16[4096,3584]{1,0:T(8,128)(2,1)} %param.18, f32[160,3584]{1,0:T(8,128)} %fusion.27, bf16[160,3584]{1,0:T(8,128)(2,1)S(1)} %copy-done.6), kind=kOutput, calls=%fused_computation.6 | convolution fusion | flops 4702289920 | bytes 38043648 | tf_op jit(solution)/shard_map/dot_general | solution.py:14
  224.9 0.0 all-reduce.2.cloned.1.call-update
  224.9 0.3 reduce-scatter.5.cloned.1.call-start
  225.2 103.0 %all-reduce.2.cloned.1.call-done = f32[160,4096]{1,0:T(8,128)} async-done(((f32[160,4096]{1,0:T(8,128)}), f32[160,4096]{1,0:T(8,128)}) %all-reduce.2.cloned.1.call-update) | async-done | bytes 2621456 | tf_op jit(solution)/shard_map/psum | solution.py:57
  328.2 0.0 copy-start.1
  328.2 2.3 fusion.14
  330.5 0.2 copy-done.1
  330.7 5.3 %fusion.21 = bf16[160,1024]{1,0:T(8,128)(2,1)S(1)} fusion(bf16[4096,1024]{1,0:T(8,128)(2,1)} %param.14, f32[1024]{0:T(1024)S(1)} %add_divide_fusion.2, bf16[160,4096]{1,0:T(8,128)(2,1)S(1)} %copy-done, f32[160,4096]{1,0:T(8,128)S(1)} %copy-done.1, f32[160]{0:T(256)S(1)} %fusion.14, f32[4096]{0:T(1024)S(1)} %convert_element_type.52, f32[160]{0:T(256)S(1)} %add_rsqrt_fusion), kind=kOutput, calls=%fused_computation.33 | convolution fusion | flops 1349058560 | bytes 12670208 | tf_op jit(solution)/shard_map/dot_general | solution.py:61
  336.0 0.0 copy-start.2
  336.1 8.3 %fusion.34 = f32[4096,1024]{1,0:T(8,128)} fusion(bf16[160,1024]{1,0:T(8,128)(2,1)S(1)} %fusion.20, bf16[160,4096]{1,0:T(8,128)(2,1)S(1)} %copy-done, f32[160,4096]{1,0:T(8,128)S(1)} %copy-done.1, f32[160]{0:T(256)S(1)} %fusion.14, f32[4096]{0:T(1024)S(1)} %convert_element_type.52, f32[160]{0:T(256)S(1)} %add_rsqrt_fusion), kind=kOutput, calls=%fused_computation.49 | convolution fusion | flops 1348730880 | bytes 21054720 | tf_op jit(solution)/shard_map/dot_general | solution.py:8
  344.4 0.0 copy-done.2
  344.4 11.4 %add_convert_fusion = bf16[4096,1024]{1,0:T(8,128)(2,1)} fusion(f32[4096,1024]{1,0:T(8,128)} %fusion.34, bf16[160,4096]{1,0:T(8,128)(2,1)S(1)} %copy-done.2, bf16[160,1024]{1,0:T(8,128)(2,1)S(1)} %fusion.21), kind=kOutput, calls=%fused_computation.1 | convolution fusion | flops 1350565888 | bytes 26804224 | tf_op jit(solution)/shard_map/dot_general | solution.py:8
  355.8 0.0 reduce-scatter.5.cloned.1.call-update
  355.8 70.9 %reduce-scatter.5.cloned.1.call-done = bf16[1024,1024]{1,0:T(8,128)(2,1)} async-done(((bf16[4096,1024]{1,0:T(8,128)(2,1)}), bf16[1024,1024]{1,0:T(8,128)(2,1)}) %reduce-scatter.5.cloned.1.call-update) | async-done | bytes 2097168 | tf_op jit(solution)/shard_map/reduce_scatter | solution.py:64
  426.7 4.1 convert_element_type.60
  (4 shorter events, 0.0 us)
Async XLA Ops:
  7.2 26.0 %copy-start.3 = (bf16[160,1024]{1,0:T(8,128)(2,1)S(1)}, bf16[160,1024]{1,0:T(8,128)(2,1)}, u32[]{:S(2)}) copy-start(bf16[160,1024]{1,0:T(8,128)(2,1)} %param.10) | copy-start | bytes 983044
  7.2 27.0 %copy-start.5 = (f32[1024]{0:T(1024)S(1)}, f32[1024]{0:T(1024)}, u32[]{:S(2)}) copy-start(f32[1024]{0:T(1024)} %param.15) | copy-start | bytes 12292
  7.2 23.3 %all-gather.4.cloned.1.call-start = ((), (), s32[]{:S(2)}) async-start(), calls=%async_computation.2 | async-start | bytes 1638400 | tf_op jit(solution)/shard_map/all_gather | solution.py:34
  7.9 59.0 %all-gather.6.cloned.1.call-start = ((), (), s32[]{:S(2)}) async-start(), calls=%async_computation.3 | async-start | bytes 1638400 | tf_op jit(solution)/shard_map/all_gather | solution.py:37
  34.1 97.3 %reduce-scatter.3.cloned.1.call-start = ((), (), s32[]{:S(2)}) async-start(), calls=%async_computation.4 | async-start | bytes 3276800 | tf_op jit(solution)/shard_map/reduce_scatter | solution.py:41
  80.1 53.4 %copy-start.4 = (bf16[4096]{0:T(1024)(128)(2,1)S(1)}, bf16[4096]{0:T(1024)(128)(2,1)}, u32[]{:S(2)}) copy-start(bf16[4096]{0:T(1024)(128)(2,1)} %param.16) | copy-start | bytes 24580
  80.1 85.7 %all-gather.8.cloned.1.call-start = ((), (), s32[]{:S(2)}) async-start(), calls=%async_computation.5 | async-start | bytes 1638400 | tf_op jit(solution)/shard_map/all_gather | solution.py:45
  133.3 194.9 %all-reduce.2.cloned.1.call-start = ((), (), s32[]{:S(2)}) async-start(), calls=%async_computation.6 | async-start | bytes 5242880 | tf_op jit(solution)/shard_map/psum | solution.py:57
  167.5 16.2 %copy-start = (bf16[160,4096]{1,0:T(8,128)(2,1)S(1)}, bf16[160,4096]{1,0:T(8,128)(2,1)}, u32[]{:S(2)}) copy-start(bf16[160,4096]{1,0:T(8,128)(2,1)} %all-gather.8.cloned.1.call-done) | copy-start | bytes 3932164
  167.5 16.2 %copy-start.6 = (bf16[160,3584]{1,0:T(8,128)(2,1)S(1)}, bf16[160,3584]{1,0:T(8,128)(2,1)}, u32[]{:S(2)}) copy-start(bf16[160,3584]{1,0:T(8,128)(2,1)} %param.19) | copy-start | bytes 3440644
  224.9 201.8 %reduce-scatter.5.cloned.1.call-start = ((), (), s32[]{:S(2)}) async-start(), calls=%async_computation.7 | async-start | bytes 10485760 | tf_op jit(solution)/shard_map/reduce_scatter | solution.py:64
  328.2 2.5 copy-start.1
  336.0 8.4 %copy-start.2 = (bf16[160,4096]{1,0:T(8,128)(2,1)S(1)}, bf16[160,4096]{1,0:T(8,128)(2,1)}, u32[]{:S(2)}) copy-start(bf16[160,4096]{1,0:T(8,128)(2,1)} %all-gather.6.cloned.1.call-done) | copy-start | bytes 3932164
Sparse Core Ops, SparseCore 0:
  9.6 20.8 all-gather.3
  34.2 32.6 all-gather.5
  80.2 51.0 reduce-scatter.2
  133.4 32.3 all-gather.7
  225.0 103.0 all-reduce.1
  355.9 70.7 reduce-scatter.4
where the time goes:
time: 438 us
  waiting for transfers between devices  312 us (71%)
  matrix products  95.6 us (22%)
  between operations  14.2 us (3%)
  other arithmetic  12.2 us (3%)
    psum x1, waiting for transfers between devices, shards(): dnormed = lax.psum(partial_grad, 'mp')  103 us
    reduce_scatter x1, waiting for transfers between devices, shards(): lax.psum_scatter((contract_first(dinter, weighted) + contract_first(diff_...  70.9 us
    reduce_scatter x1, waiting for transfers between devices, shards(): lax.psum_scatter(contract_last(rotation, weighted), 'mp', scatter_dimensi...  51.2 us
    dot_general x3, matrix products, contract_last(): lax.dot_general(left, right, (((1,), (1,)), ((), ())), preferred_element_...  49 us
    all_gather x1, waiting for transfers between devices, shards(): diff_full = lax.all_gather(diff_local, 'mp', axis=1, tiled=True)  32.8 us
    all_gather x1, waiting for transfers between devices, shards(): full_rows = lax.all_gather(interchanged, 'mp', axis=1, tiled=True)  32.3 us
    all_gather x1, waiting for transfers between devices, shards(): everyone = lax.all_gather(source_states, 'dp', axis=0, tiled=True)  21.2 us
    dot_general x2, matrix products, contract_first(): lax.dot_general(left, right, (((0,), (0,)), ((), ())), preferred_element_...  19.7 us
  transfers between devices with their start and end apart: 6, of which 6 were waited for; matrix products, arithmetic and copies ran while one was open for 0% of the time, Pallas kernels for 0%

commit v1 on v0

--- a/solution.py
+++ b/solution.py
@@ -54,7 +54,7 @@
     dgate = (cotan * up_val * sigm * (1.0 + gate * (1.0 - sigm))).astype(jnp.bfloat16)
     dup_val = (cotan * gate * sigm).astype(jnp.bfloat16)
     partial_grad = contract_last(dgate, gate_weight) + contract_last(dup_val, up_weight)
-    dnormed = lax.psum(partial_grad, "mp")
+    dnormed = jnp.sum(lax.all_gather(partial_grad, "mp"), axis=0)
     scaled = gain_f * dnormed
     stat = jnp.sum(scaled * states, axis=1, keepdims=True)
     dinter = (recip * scaled - states * recip * recip * recip * stat / width).astype(jnp.bfloat16)

time: 438 us -> 522 us (1.19)
  waiting for transfers between devices: 312 us -> 391 us
    all_gather x0 -> x1, waiting for transfers between devices: none -> 183 us  [shards(): dnormed = jnp.sum(lax.all_gather(partial_grad, 'mp'), axis=0)]
    psum x1 -> x0, waiting for transfers between devices: 103 us -> none  [shards(): dnormed = lax.psum(partial_grad, 'mp')]
where the time goes in v1:
time: 522 us; the launch traced here: 521 us
  waiting for transfers between devices  391 us (75%)
  matrix products  95.5 us (18%)
  other arithmetic  16.9 us (3%)
  between operations  14.2 us (3%)
    all_gather x1, waiting for transfers between devices, shards(): dnormed = jnp.sum(lax.all_gather(partial_grad, 'mp'), axis=0)  183 us
    reduce_scatter x1, waiting for transfers between devices, shards(): lax.psum_scatter((contract_first(dinter, weighted) + contract_first(diff_...  70.1 us
    reduce_scatter x1, waiting for transfers between devices, shards(): lax.psum_scatter(contract_last(rotation, weighted), 'mp', scatter_dimensi...  51.2 us
    dot_general x3, matrix products, contract_last(): lax.dot_general(left, right, (((1,), (1,)), ((), ())), preferred_element_...  48.9 us
    all_gather x1, waiting for transfers between devices, shards(): diff_full = lax.all_gather(diff_local, 'mp', axis=1, tiled=True)  32.8 us
    all_gather x1, waiting for transfers between devices, shards(): full_rows = lax.all_gather(interchanged, 'mp', axis=1, tiled=True)  32.3 us
    all_gather x1, waiting for transfers between devices, shards(): everyone = lax.all_gather(source_states, 'dp', axis=0, tiled=True)  21.2 us
    dot_general x2, matrix products, contract_first(): lax.dot_general(left, right, (((0,), (0,)), ((), ())), preferred_element_...  19.7 us
  transfers between devices with their start and end apart: 6, of which 6 were waited for; matrix products, arithmetic and copies ran while one was open for 0% of the time, Pallas kernels for 0%

profile of v1, /device:TPU:0, one launch (start us, length us, event | category | flops | bytes accessed | tf_op | source)
XLA Modules:
  0.0 521.0 jit_solution(2216762580217959727)
XLA Ops:
  7.2 0.0 copy-start.3
  7.2 0.0 copy-start.5
  7.2 0.0 all-gather.6.cloned.1.call-start
  7.2 0.7 all-gather.6.cloned.1.call-update
  7.9 0.0 all-gather.8.cloned.1.call-start
  8.0 0.7 broadcast_multiply_fusion
  8.6 0.7 compare_and_fusion
  9.3 21.2 %all-gather.6.cloned.1.call-done = bf16[640,1024]{1,0:T(8,128)(2,1)} async-done(((bf16[160,1024]{1,0:T(8,128)(2,1)}), bf16[640,1024]{1,0:T(8,128)(2,1)}) %all-gather.6.cloned.1.call-update) | async-done | bytes 1310736 | tf_op jit(solution)/shard_map/all_gather | solution.py:34
  30.5 2.7 gather_fusion
  33.2 0.0 copy-done.3
  33.2 0.9 fusion.25
  34.1 0.0 all-gather.8.cloned.1.call-update
  34.1 0.0 reduce-scatter.3.cloned.1.call-start
  34.1 0.0 copy-done.5
  34.2 32.8 %all-gather.8.cloned.1.call-done = bf16[160,4096]{1,0:T(8,128)(2,1)} async-done(((bf16[160,1024]{1,0:T(8,128)(2,1)}), bf16[160,4096]{1,0:T(8,128)(2,1)}) %all-gather.8.cloned.1.call-update) | async-done | bytes 1310736 | tf_op jit(solution)/shard_map/all_gather | solution.py:37
  66.9 5.3 %fusion.20 = bf16[160,1024]{1,0:T(8,128)(2,1)S(1)} fusion(bf16[160,4096]{1,0:T(8,128)(2,1)} %all-gather.8.cloned.1.call-done, bf16[4096,1024]{1,0:T(8,128)(2,1)} %param.14, f32[1024]{0:T(1024)S(1)} %add_divide_fusion.2), kind=kOutput, calls=%fused_computation.32 | convolution fusion | flops 1342504960 | bytes 10031104 | tf_op jit(solution)/shard_map/dot_general | solution.py:39
  72.3 7.8 %convolution_bitcast_fusion = f32[4096,160]{0,1:T(8,128)} fusion(bf16[160,1024]{1,0:T(8,128)(2,1)S(1)} %fusion.20, bf16[4096,1024]{1,0:T(8,128)(2,1)} %param.14), kind=kOutput, calls=%fused_computation.5 | convolution fusion | flops 1342177280 | bytes 11337728 | tf_op jit(solution)/shard_map/dot_general | solution.py:14
  80.1 0.0 copy-start.4
  80.1 0.0 reduce-scatter.3.cloned.1.call-update
  80.1 0.0 all-gather.10.cloned.1.call-start
  80.1 51.2 %reduce-scatter.3.cloned.1.call-done = f32[1024,160]{0,1:T(8,128)} async-done(((f32[4096,160]{0,1:T(8,128)}), f32[1024,160]{0,1:T(8,128)}) %reduce-scatter.3.cloned.1.call-update) | async-done | bytes 655376 | tf_op jit(solution)/shard_map/reduce_scatter | solution.py:41
  131.3 1.9 fusion.26
  133.2 0.0 all-gather.10.cloned.1.call-update
  133.3 0.2 all-gather.12.cloned.1.call-start
  133.5 0.0 copy-done.4
  133.5 32.3 %all-gather.10.cloned.1.call-done = bf16[160,4096]{1,0:T(8,128)(2,1)} async-done(((bf16[160,1024]{1,0:T(8,128)(2,1)}), bf16[160,4096]{1,0:T(8,128)(2,1)}) %all-gather.10.cloned.1.call-update) | async-done | bytes 1310736 | tf_op jit(solution)/shard_map/all_gather | solution.py:45
  165.8 1.7 fusion.13
  167.5 0.0 copy-start.6
  167.5 16.2 %fusion.27 = f32[160,3584]{1,0:T(8,128)} fusion(bf16[4096,3584]{1,0:T(8,128)(2,1)} %param.17, bf16[160,4096]{1,0:T(8,128)(2,1)} %all-gather.10.cloned.1.call-done, f32[4096]{0:T(1024)S(1)} %convert_element_type.52, f32[160]{0:T(256)S(1)} %add_rsqrt_fusion), kind=kOutput, calls=%fused_computation.40 | convolution fusion | flops 4700241920 | bytes 32981632 | tf_op jit(solution)/shard_map/dot_general | solution.py:50
  183.7 0.0 copy-done
  183.7 0.0 copy-done.6
  183.7 25.1 %fusion.3 = f32[160,4096]{1,0:T(8,128)} fusion(bf16[4096,3584]{1,0:T(8,128)(2,1)} %param.17, bf16[4096,3584]{1,0:T(8,128)(2,1)} %param.18, bf16[160,3584]{1,0:T(8,128)(2,1)S(1)} %copy-done.6, f32[160,3584]{1,0:T(8,128)} %fusion.27, bf16[160,4096]{1,0:T(8,128)(2,1)S(1)} %copy-done, f32[4096]{0:T(1024)S(1)} %convert_element_type.52, f32[160]{0:T(256)S(1)} %add_rsqrt_fusion), kind=kOutput, calls=%fused_computation.11 | convolution fusion | flops 9404170240 | bytes 66110080 | tf_op jit(solution)/shard_map/dot_general | solution.py:14
  208.8 16.1 %convolution_add_fusion = f32[160,4096]{1,0:T(8,128)} fusion(f32[160,4096]{1,0:T(8,128)} %fusion.3, bf16[4096,3584]{1,0:T(8,128)(2,1)} %param.18, f32[160,3584]{1,0:T(8,128)} %fusion.27, bf16[160,3584]{1,0:T(8,128)(2,1)S(1)} %copy-done.6), kind=kOutput, calls=%fused_computation.6 | convolution fusion | flops 4702289920 | bytes 38043648 | tf_op jit(solution)/shard_map/dot_general | solution.py:14
  224.9 0.0 all-gather.12.cloned.1.call-update
  224.9 0.3 reduce-scatter.5.cloned.1.call-start
  225.1 182.8 %all-gather.12.cloned.1.call-done = f32[640,4096]{1,0:T(8,128)} async-done(((f32[160,4096]{1,0:T(8,128)}), f32[640,4096]{1,0:T(8,128)}) %all-gather.12.cloned.1.call-update) | async-done | bytes 10485776 | tf_op jit(solution)/shard_map/all_gather | solution.py:57
  408.0 5.1 reduce_sum.28
  413.1 0.0 copy-start.1
  413.1 1.8 fusion.14
  414.9 0.0 copy-done.1
  414.9 5.3 %fusion.21 = bf16[160,1024]{1,0:T(8,128)(2,1)S(1)} fusion(bf16[4096,1024]{1,0:T(8,128)(2,1)} %param.14, f32[1024]{0:T(1024)S(1)} %add_divide_fusion.2, bf16[160,4096]{1,0:T(8,128)(2,1)S(1)} %copy-done.1, f32[160,4096]{1,0:T(8,128)S(1)} %reduce_sum.28, f32[160]{0:T(256)S(1)} %fusion.14, f32[4096]{0:T(1024)S(1)} %convert_element_type.52, ...), kind=kOutput, calls=%fused_computation.33 | convolution fusion | flops 1349058560 | bytes 12670208 | tf_op jit(solution)/shard_map/dot_general | solution.py:61
  420.3 0.0 copy-start.2
  420.3 8.3 %fusion.34 = f32[4096,1024]{1,0:T(8,128)} fusion(bf16[160,1024]{1,0:T(8,128)(2,1)S(1)} %fusion.20, bf16[160,4096]{1,0:T(8,128)(2,1)S(1)} %copy-done.1, f32[160,4096]{1,0:T(8,128)S(1)} %reduce_sum.28, f32[160]{0:T(256)S(1)} %fusion.14, f32[4096]{0:T(1024)S(1)} %convert_element_type.52, f32[160]{0:T(256)S(1)} %add_rsqrt_fusion), kind=kOutput, calls=%fused_computation.49 | convolution fusion | flops 1348730880 | bytes 21054720 | tf_op jit(solution)/shard_map/dot_general | solution.py:8
  428.6 0.0 copy-done.2
  428.6 11.4 %add_convert_fusion = bf16[4096,1024]{1,0:T(8,128)(2,1)} fusion(f32[4096,1024]{1,0:T(8,128)} %fusion.34, bf16[160,4096]{1,0:T(8,128)(2,1)S(1)} %copy-done.2, bf16[160,1024]{1,0:T(8,128)(2,1)S(1)} %fusion.21), kind=kOutput, calls=%fused_computation.1 | convolution fusion | flops 1350565888 | bytes 26804224 | tf_op jit(solution)/shard_map/dot_general | solution.py:8
  440.0 0.0 reduce-scatter.5.cloned.1.call-update
  440.0 70.1 %reduce-scatter.5.cloned.1.call-done = bf16[1024,1024]{1,0:T(8,128)(2,1)} async-done(((bf16[4096,1024]{1,0:T(8,128)(2,1)}), bf16[1024,1024]{1,0:T(8,128)(2,1)}) %reduce-scatter.5.cloned.1.call-update) | async-done | bytes 2097168 | tf_op jit(solution)/shard_map/reduce_scatter | solution.py:64
  510.1 4.1 convert_element_type.60
  (5 shorter events, 0.0 us)
Async XLA Ops:
  7.2 26.0 %copy-start.3 = (bf16[160,1024]{1,0:T(8,128)(2,1)S(1)}, bf16[160,1024]{1,0:T(8,128)(2,1)}, u32[]{:S(2)}) copy-start(bf16[160,1024]{1,0:T(8,128)(2,1)} %param.10) | copy-start | bytes 983044
  7.2 27.0 %copy-start.5 = (f32[1024]{0:T(1024)S(1)}, f32[1024]{0:T(1024)}, u32[]{:S(2)}) copy-start(f32[1024]{0:T(1024)} %param.15) | copy-start | bytes 12292
  7.2 23.3 %all-gather.6.cloned.1.call-start = ((), (), s32[]{:S(2)}) async-start(), calls=%async_computation.2 | async-start | bytes 1638400 | tf_op jit(solution)/shard_map/all_gather | solution.py:34
  7.9 59.0 %all-gather.8.cloned.1.call-start = ((), (), s32[]{:S(2)}) async-start(), calls=%async_computation.3 | async-start | bytes 1638400 | tf_op jit(solution)/shard_map/all_gather | solution.py:37
  34.1 97.3 %reduce-scatter.3.cloned.1.call-start = ((), (), s32[]{:S(2)}) async-start(), calls=%async_computation.4 | async-start | bytes 3276800 | tf_op jit(solution)/shard_map/reduce_scatter | solution.py:41
  80.1 53.4 %copy-start.4 = (bf16[4096]{0:T(1024)(128)(2,1)S(1)}, bf16[4096]{0:T(1024)(128)(2,1)}, u32[]{:S(2)}) copy-start(bf16[4096]{0:T(1024)(128)(2,1)} %param.16) | copy-start | bytes 24580
  80.1 85.7 %all-gather.10.cloned.1.call-start = ((), (), s32[]{:S(2)}) async-start(), calls=%async_computation.5 | async-start | bytes 1638400 | tf_op jit(solution)/shard_map/all_gather | solution.py:45
  133.3 274.7 %all-gather.12.cloned.1.call-start = ((), (), s32[]{:S(2)}) async-start(), calls=%async_computation.7 | async-start | bytes 13107200 | tf_op jit(solution)/shard_map/all_gather | solution.py:57
  167.5 16.2 %copy-start = (bf16[160,4096]{1,0:T(8,128)(2,1)S(1)}, bf16[160,4096]{1,0:T(8,128)(2,1)}, u32[]{:S(2)}) copy-start(bf16[160,4096]{1,0:T(8,128)(2,1)} %all-gather.10.cloned.1.call-done) | copy-start | bytes 3932164
  167.5 16.2 %copy-start.6 = (bf16[160,3584]{1,0:T(8,128)(2,1)S(1)}, bf16[160,3584]{1,0:T(8,128)(2,1)}, u32[]{:S(2)}) copy-start(bf16[160,3584]{1,0:T(8,128)(2,1)} %param.19) | copy-start | bytes 3440644
  224.9 285.2 %reduce-scatter.5.cloned.1.call-start = ((), (), s32[]{:S(2)}) async-start(), calls=%async_computation.6 | async-start | bytes 10485760 | tf_op jit(solution)/shard_map/reduce_scatter | solution.py:64
  413.1 1.9 copy-start.1
  420.3 8.3 %copy-start.2 = (bf16[160,4096]{1,0:T(8,128)(2,1)S(1)}, bf16[160,4096]{1,0:T(8,128)(2,1)}, u32[]{:S(2)}) copy-start(bf16[160,4096]{1,0:T(8,128)(2,1)} %all-gather.8.cloned.1.call-done) | copy-start | bytes 3932164
Sparse Core Ops, SparseCore 0:
  9.6 20.8 all-gather.5
  34.2 32.6 all-gather.7
  80.2 51.0 reduce-scatter.2
  133.4 32.3 all-gather.9
  225.0 182.9 all-gather.11
  440.1 69.9 reduce-scatter.4
